TPU v7x, 128 devices: a whole 4x4x4 slice. The times are simulated.
128 devices in a mesh: head: 2 (over y_hi), seq: 64 (over z, x, y_lo, core).
Axes of the slice: x: 4, y: 4 (y_hi: 2, y_lo: 2; y = y_hi * 2 + y_lo), z: 4, core: 2. Of those that a mesh axis runs over, the one named last changes fastest.
Arguments:
- queries: bfloat16 [65536, 2048], P('seq', 'head'), may hold values from -24 to 24
- key_rows: bfloat16 [65536, 2048], P('seq', 'head'), may hold values from -24 to 24
- value_rows: bfloat16 [65536, 2048], P('seq', 'head'), may hold values from -6 to 6
- token_rates: float32 [4, 65536], P('head', 'seq'), may hold values from 0.01 to 1
- gate_fast: float32 [4, 512, 512], P('head'), may hold values from -0.25 to 0.25
- lift_fast: float32 [4, 512, 512], P('head'), may hold values from -0.25 to 0.25
- down_fast: float32 [4, 512, 512], P('head'), may hold values from -0.25 to 0.25
- memory_gain: float32 [4, 512], P('head'), may hold values from 0.1 to 1
- out_weight: bfloat16 [2048, 2048], P('head'), may hold values from -0.125 to 0.125
Outputs:
- layer_out: bfloat16 [65536, 2048], P('seq', 'head')
All inputs are finite; a program needn't handle non-finite values.
Results may differ from a plain program's by a relative error of at most 0.014.
Values may be sent and summed in bfloat16 or wider, within the bound.
No kernel may reach another device: no remote copies, remote signals or barrier semaphores. Data moves between devices by JAX's collectives and lax.ppermute only.
A program may use at most 128 MiB of HBM per device.

v0:
```python
import jax
import jax.numpy as jnp
from jax import lax
from jax.sharding import PartitionSpec as P

HEAD = 512
WINDOW = 1024
NS_STEPS = 2


COEF_A = 3.4445
COEF_B = -4.775
COEF_C = 2.0315
EPSILON = 1e-06


def shifted(value, axis, steps):
    count = lax.axis_size(axis)
    initial, last = (max(0, -steps), min(count, count - steps))
    return lax.ppermute(value, axis, [(source, source + steps) for source in range(initial, last)])


def split_up(x, dim, count):
    dims = x.shape
    tiles = x.reshape(*dims[:dim], count, dims[dim] // count, *dims[dim + 1 :])
    return jnp.moveaxis(tiles, dim, 0)


def summed_on_arrival(x, axis, dim):
    tiles = split_up(x, dim, lax.axis_size(axis))
    arrived = lax.all_to_all(tiles, axis, split_axis=0, concat_axis=0, tiled=True)
    return arrived.astype(jnp.float32).sum(axis=0)


def window_attention(queries, key_rows, value_rows, edge_keys, edge_values, offset):
    tokens_here = queries.shape[0]
    width_here = queries.shape[1]
    heads_here = width_here // HEAD
    block_rows = min(512, tokens_here)
    span_rows = block_rows + WINDOW
    all_keys = jnp.concatenate([edge_keys, key_rows], axis=0)
    all_values = jnp.concatenate([edge_values, value_rows], axis=0)
    score_scale = HEAD ** (-0.5)
    query_index = jnp.arange(block_rows, dtype=jnp.int32)[:, None]
    key_index = jnp.arange(span_rows, dtype=jnp.int32)[None, :]

    def one_block(start):
        query_block = lax.dynamic_slice_in_dim(queries, start, block_rows, 0).reshape(
            block_rows, heads_here, HEAD
        )
        key_block = lax.dynamic_slice_in_dim(all_keys, start, span_rows, 0).reshape(
            span_rows, heads_here, HEAD
        )
        value_block = lax.dynamic_slice_in_dim(all_values, start, span_rows, 0).reshape(
            span_rows, heads_here, HEAD
        )
        scores = (
            jnp.einsum("qhd,khd->hqk", query_block, key_block, preferred_element_type=jnp.float32)
            * score_scale
        )
        allowed = (
            (key_index > query_index)
            & (key_index <= query_index + WINDOW)
            & (offset + start + key_index - WINDOW >= 0)
        )
        scores = jnp.where(allowed[None, :, :], scores, -jnp.inf)
        largest = jnp.max(scores, axis=2, keepdims=True)
        exponent = jnp.exp(scores - largest)
        probability = (exponent / jnp.sum(exponent, axis=2, keepdims=True)).astype(jnp.bfloat16)
        attended = jnp.einsum(
            "hqk,khd->qhd", probability, value_block, preferred_element_type=jnp.float32
        )
        return attended.reshape(block_rows, width_here)

    starts = jnp.arange(tokens_here // block_rows, dtype=jnp.int32) * block_rows
    return lax.map(one_block, starts).reshape(tokens_here, width_here)


def fast_gradients(key_heads, value_heads, rate_rows, gate_fast, lift_fast, down_fast):
    gate_pre = jnp.einsum(
        "thd,hdf->thf",
        key_heads,
        gate_fast.astype(jnp.bfloat16),
        preferred_element_type=jnp.float32,
    )
    lift_pre = jnp.einsum(
        "thd,hdf->thf",
        key_heads,
        lift_fast.astype(jnp.bfloat16),
        preferred_element_type=jnp.float32,
    )
    sigmoid_gate = jax.nn.sigmoid(gate_pre)
    activated = gate_pre * sigmoid_gate
    hidden = (activated * lift_pre).astype(jnp.bfloat16)
    target = (-rate_rows[:, :, None] * value_heads).astype(jnp.bfloat16)
    grad_down = jnp.einsum("thf,thd->hfd", hidden, target, preferred_element_type=jnp.float32)
    back_hidden = jnp.einsum(
        "thd,hfd->thf", target, down_fast.astype(jnp.bfloat16), preferred_element_type=jnp.float32
    )
    back_gate = (
        back_hidden * lift_pre * sigmoid_gate * (1.0 + gate_pre * (1.0 - sigmoid_gate))
    ).astype(jnp.bfloat16)
    back_lift = (back_hidden * activated).astype(jnp.bfloat16)
    grad_gate = jnp.einsum("thd,thf->hdf", key_heads, back_gate, preferred_element_type=jnp.float32)
    grad_lift = jnp.einsum("thd,thf->hdf", key_heads, back_lift, preferred_element_type=jnp.float32)
    return (grad_gate, grad_lift, grad_down)


def orthogonalize(gradient):
    column_gram = jnp.einsum("hrc,hrd->hcd", gradient, gradient)
    trace_sum = jnp.trace(column_gram, axis1=1, axis2=2) + EPSILON
    iterate = (gradient / jnp.sqrt(trace_sum)[:, None, None]).astype(jnp.bfloat16)
    column_gram = column_gram / trace_sum[:, None, None]
    identity = jnp.eye(column_gram.shape[1], dtype=jnp.float32)
    for sweep_index in range(NS_STEPS):
        gram_half = column_gram.astype(jnp.bfloat16)
        square = jnp.einsum(
            "hcd,hde->hce", gram_half, gram_half, preferred_element_type=jnp.float32
        )
        polynomial = (COEF_A * identity + COEF_B * column_gram + COEF_C * square).astype(
            jnp.bfloat16
        )
        iterate = jnp.einsum(
            "hrc,hcd->hrd", iterate, polynomial, preferred_element_type=jnp.float32
        ).astype(jnp.bfloat16)
        if sweep_index + 1 < NS_STEPS:
            column_gram = jnp.einsum(
                "hrc,hrd->hcd", iterate, iterate, preferred_element_type=jnp.float32
            )
    return iterate


def renew(old_weight, update):
    change = old_weight - update.astype(jnp.float32)
    old_square = jnp.sum(old_weight * old_weight, axis=1, keepdims=True)
    new_square = jnp.sum(change * change, axis=1, keepdims=True)
    return (change * jnp.sqrt(old_square / (new_square + EPSILON))).astype(jnp.bfloat16)


def shards(
    queries,
    key_rows,
    value_rows,
    token_rates,
    gate_fast,
    lift_fast,
    down_fast,
    memory_gain,
    out_weight,
):
    tokens_here = queries.shape[0]
    heads_here = gate_fast.shape[0]
    edge_keys, edge_values = shifted((key_rows, value_rows), "seq", 1)
    offset = lax.axis_index("seq") * tokens_here
    attended = window_attention(queries, key_rows, value_rows, edge_keys, edge_values, offset)
    key_heads = key_rows.reshape(tokens_here, heads_here, HEAD)
    value_heads = value_rows.reshape(tokens_here, heads_here, HEAD)
    rate_rows = token_rates.T
    grad_gate, grad_lift, grad_down = fast_gradients(
        key_heads, value_heads, rate_rows, gate_fast, lift_fast, down_fast
    )
    summed_gate, summed_lift, summed_down = lax.psum((grad_gate, grad_lift, grad_down), "seq")
    stacked = jnp.concatenate([summed_gate, summed_lift, summed_down], axis=0)
    ortho_all = orthogonalize(stacked)
    ortho_gate = ortho_all[:heads_here]
    ortho_lift = ortho_all[heads_here : 2 * heads_here]
    ortho_down = ortho_all[2 * heads_here :]
    gate_new = renew(gate_fast, ortho_gate)
    lift_new = renew(lift_fast, ortho_lift)
    down_new = renew(down_fast, ortho_down)
    query_heads = queries.reshape(tokens_here, heads_here, HEAD)
    gate_apply = jnp.einsum(
        "thd,hdf->thf", query_heads, gate_new, preferred_element_type=jnp.float32
    )
    lift_apply = jnp.einsum(
        "thd,hdf->thf", query_heads, lift_new, preferred_element_type=jnp.float32
    )
    hidden_apply = (jax.nn.silu(gate_apply) * lift_apply).astype(jnp.bfloat16)
    memory_out = jnp.einsum(
        "thf,hfd->thd", hidden_apply, down_new, preferred_element_type=jnp.float32
    )
    mean_square = jnp.mean(memory_out * memory_out, axis=2, keepdims=True)
    normed = memory_out * lax.rsqrt(mean_square + EPSILON) * memory_gain[None, :, :]
    combined = (
        (attended.reshape(tokens_here, heads_here, HEAD) + normed)
        .astype(jnp.bfloat16)
        .reshape(tokens_here, heads_here * HEAD)
    )
    partial_out = jnp.dot(combined, out_weight, preferred_element_type=jnp.float32)
    projected = summed_on_arrival(partial_out.astype(jnp.bfloat16), "head", 1)
    return projected.astype(jnp.bfloat16)


def solution(mesh):
    return jax.shard_map(
        shards,
        mesh=mesh,
        in_specs=(
            P("seq", "head"),
            P("seq", "head"),
            P("seq", "head"),
            P("head", "seq"),
            P("head", None, None),
            P("head", None, None),
            P("head", None, None),
            P("head", None),
            P("head", None),
        ),
        out_specs=P("seq", "head"),
        check_vma=False,
    )
```

profile of v0, /device:TPU:0, one launch (start us, length us, event | category | flops | bytes accessed | tf_op | source)
XLA Modules:
  0.0 749.4 jit_solution(6871751844328882870)
XLA Ops:
  6.5 4.1 copy.63
  10.6 2.7 collective-permute-start
  13.3 2.6 copy.65
  15.9 4.4 collective-permute-start.1
  20.3 2.0 convert_element_type.110
  22.4 0.0 copy-start.10
  22.4 1.3 fusion.77
  23.7 0.3 copy-done.10
  24.0 1.3 fusion.75
  25.3 0.3 copy-done.9
  25.6 1.3 fusion.105
  26.9 3.4 fusion.67
  30.3 3.0 fusion.87
  33.3 3.4 fusion.82
  36.7 0.0 all-reduce.3.cloned.1.call-update
  36.7 0.1 iota_compare_fusion.2
  36.8 1.1 broadcast_select_fusion
  37.9 0.7 copy-done.8
  38.7 4.0 pad_maximum_fusion
  42.7 4.0 pad_maximum_fusion.1
  46.7 155.9 %while.14 = (s32[]{:T(128)}, f32[2,512,1024]{1,0,2:T(2,128)}, s32[2]{0:T(128)S(1)}, bf16[2048,1024]{0,1:T(8,128)(2,1)}, s32[]{:T(128)}, /*index=5*/bf16[1024,102...) while((s32[]{:T(128)}, f32[2,512,1024]{1,0,2:T(2,128)}, ...), condition=%wide.region_3.4_spmd.clone.clone, body=%wide.region_0.3_spmd.clone.clone.sunk | while | flops 3238536192 | bytes 71580944 | solution.py:76
  47.2 0.6 dynamic_slice.41
  49.5 8.1 %constant_dynamic-slice_fusion.5 = (bf16[1536,1024]{0,1:T(8,128)(2,1)S(1)}, bf16[1536,1024]{0,1:T(8,128)(2,1)}) fusion(bf16[2048,1024]{0,1:T(8,128)(2,1)} %get-tuple-element.283, s32[]{:T(128)S(6)} %select_n.49, bf16[2048,1024]{0,1:T(8,128)(2,1)} %get-tuple-element.280), kind=kLoop, calls=%fused_computation.19.clone.1 | loop fusion | bytes 12582916 | tf_op jit(solution)/shard_map/while/body/eval_jaxpr/dynamic_slice | solution.py:51
  58.7 2.5 constant_dynamic-slice_fusion.6
  61.2 2.3 copy.161
  63.5 5.7 fusion.151
  69.8 0.6 fusion.153
  70.4 0.9 copy-done.3
  71.3 5.0 fusion.154
  76.3 7.2 fusion.155
  83.5 3.7 copy.162
  87.2 37.7 %dynamic_update_slice.10 = f32[2,512,1024]{1,0,2:T(2,128)} dynamic-update-slice(f32[2,512,1024]{1,0,2:T(2,128)} %get-tuple-element.267, f32[1,512,1024]{1,0,2:T(1,128)S(1)} %copy.162, s32[]{:T(128)S(6)} %copy.166, s32[]{:T(128)} %constant.73.clone.1..sunk, s32[]{:T(128)} %constant.73.clone.1..sunk) | dynamic-update-slice | bytes 4194308 | tf_op jit(solution)/shard_map/while/body/jit(dynamic_update_index_in_dim)/dynamic_update_slice | solution.py:76
  124.9 0.6 dynamic_slice.41
  127.2 7.9 %constant_dynamic-slice_fusion.5 = (bf16[1536,1024]{0,1:T(8,128)(2,1)S(1)}, bf16[1536,1024]{0,1:T(8,128)(2,1)}) fusion(bf16[2048,1024]{0,1:T(8,128)(2,1)} %get-tuple-element.283, s32[]{:T(128)S(6)} %select_n.49, bf16[2048,1024]{0,1:T(8,128)(2,1)} %get-tuple-element.280), kind=kLoop, calls=%fused_computation.19.clone.1 | loop fusion | bytes 12582916 | tf_op jit(solution)/shard_map/while/body/eval_jaxpr/dynamic_slice | solution.py:51
  136.3 2.5 constant_dynamic-slice_fusion.6
  138.8 2.3 copy.161
  141.1 5.7 fusion.151
  147.3 0.6 fusion.153
  148.0 0.9 copy-done.3
  148.9 5.1 fusion.154
  153.9 7.1 fusion.155
  161.0 3.8 copy.162
  164.8 37.7 %dynamic_update_slice.10 = f32[2,512,1024]{1,0,2:T(2,128)} dynamic-update-slice(f32[2,512,1024]{1,0,2:T(2,128)} %get-tuple-element.267, f32[1,512,1024]{1,0,2:T(1,128)S(1)} %copy.162, s32[]{:T(128)S(6)} %copy.166, s32[]{:T(128)} %constant.73.clone.1..sunk, s32[]{:T(128)} %constant.73.clone.1..sunk) | dynamic-update-slice | bytes 4194308 | tf_op jit(solution)/shard_map/while/body/jit(dynamic_update_index_in_dim)/dynamic_update_slice | solution.py:76
  202.6 6.6 reshape_reshape.3
  209.3 408.9 %all-reduce.3.cloned.1.call-done = (f32[2,512,512]{1,2,0:T(8,128)}, f32[2,512,512]{1,2,0:T(8,128)}, f32[2,512,512]{1,2,0:T(8,128)}) async-done(((f32[2,512,512]{1,2,0:T(8,128)}, f32[2,512,512]{1,2,0:T(8,128)}, f32[2,512,512]{1,2,0:T(8,128)}), (f32[2,512,512]{1,2,0:T(8,128)}, f32[2,512,512]{1,2,0:T(8,128)}, f32[2,512,512]{1,2,0:T(8,128)})) %all-reduce.3.cloned.1.call-update) | async-done | bytes 6291472 | tf_op jit(solution)/shard_map/psum | solution.py:162
  618.2 1.9 constant_dynamic-update-slice_fusion.2
  620.1 0.3 copy-done.12
  620.4 0.2 constant_dynamic-update-slice_fusion.1
  620.6 0.5 copy-done.11
  621.1 0.2 constant_dynamic-update-slice_fusion
  621.2 4.7 select_reduce_fusion
  625.9 12.5 %fusion.62 = bf16[6,512,512]{2,1,0:T(8,128)(2,1)S(1)} fusion(f32[512,512]{1,0:T(8,128)} %broadcast_select_fusion, f32[6,512,512]{2,1,0:T(8,128)} %get-tuple-element.203, f32[6]{0:T(128)S(1)} %get-tuple-element.201, f32[6,512,512]{1,2,0:T(8,128)} %copy-done.1, f32[6]{0:T(128)S(1)} %get-tuple-element.200), kind=kOutput, calls=%fused_computation.79 | convolution fusion | flops 3238526976 | bytes 16777264 | tf_op jit(solution)/shard_map/hrc,hcd->hrd/dot_general | solution.py:123
  638.4 4.5 fusion.129
  642.9 12.7 %fusion.59 = bf16[6,512,512]{2,1,0:T(8,128)(2,1)} fusion(bf16[6,512,512]{2,1,0:T(8,128)(2,1)S(1)} %fusion.62, f32[6,512,512]{2,1,0:T(8,128)} %fusion.129, f32[512,512]{1,0:T(8,128)} %broadcast_select_fusion), kind=kOutput, calls=%fused_computation.78 | convolution fusion | flops 3232235520 | bytes 13631488 | tf_op jit(solution)/shard_map/hrc,hcd->hrd/dot_general | solution.py:123
  655.6 4.7 multiply_reduce_fusion.4
  660.4 0.2 copy-done.6
  660.6 4.5 fusion.69
  665.2 9.1 %fusion.21 = (f32[1024,2]{0,1:T(2,128)S(1)}, f32[2,512,1024]{2,1,0:T(8,128)}) fusion(f32[2,512,1024]{1,2,0:T(8,128)} %fusion.69, bf16[128,2,8,512]{3,2,1,0:T(8,128)(2,1)S(1)} %bitcast.174, f32[2,512,512]{2,1,0:T(8,128)} %param.16, f32[2,512]{1,0:T(2,128)S(1)} %fusion.115, bf16[6,512,512]{2,1,0:T(8,128)(2,1)} %fusion.59, f32[2,512,512]{2,1,0:T(8,128)} %param.17, ...), kind=kOutput, calls=%fused_computation.37 | convolution fusion | flops 2160064512 | bytes 16793600 | tf_op jit(solution)/shard_map/thf,hfd->thd/dot_general | solution.py:179
  674.3 4.2 fusion.24
  678.5 0.5 copy-done.15
  678.9 4.9 convolution_convert_fusion
  683.8 0.5 copy.158
  684.4 52.8 %all_to_all.5 = bf16[2,1024,1024]{2,1,0:T(8,128)(2,1)} all-to-all(bf16[2,1024,1024]{2,1,0:T(8,128)(2,1)S(1)} %bitcast.181), channel_id=1, replica_groups=mesh['head'=2,'seq'=64] {'head'}, dimensions={0} | all-to-all | bytes 8388608 | tf_op jit(solution)/shard_map/all_to_all | solution.py:31
  737.2 5.2 reduce_sum.105
  (40 shorter events, 0.1 us)
Async XLA Ops:
  6.5 6.7 copy-start.4
  6.5 611.7 %all-reduce.3.cloned.1.call-start = ((), (), s32[]{:S(2)}) async-start(), calls=%async_computation.1 | async-start | bytes 12582912 | tf_op jit(solution)/shard_map/psum | solution.py:162
  10.6 27.3 %collective-permute-start = (bf16[1024,1024]{0,1:T(8,128)(2,1)}, bf16[1024,1024]{0,1:T(8,128)(2,1)}, u32[]{:S(2)}, u32[]{:S(2)}) collective-permute-start(bf16[1024,1024]{0,1:T(8,128)(2,1)} %copy.63), channel_id=1, source_target_pairs={{0,1},{1,2},{2,3},{3,4},{4,5},{5,6},{6,7},{7,8},{8,9},{9,10},{10,1... | collective-permute-start | bytes 6291464 | tf_op jit(solution)/shard_map/ppermute | solution.py:20
  15.9 6.5 copy-start.5
  15.9 26.8 %collective-permute-start.1 = (bf16[1024,1024]{0,1:T(8,128)(2,1)}, bf16[1024,1024]{0,1:T(8,128)(2,1)}, u32[]{:S(2)}, u32[]{:S(2)}) collective-permute-start(bf16[1024,1024]{0,1:T(8,128)(2,1)} %copy.65), channel_id=1, source_target_pairs={{0,1},{1,2},{2,3},{3,4},{4,5},{5,6},{6,7},{7,8},{8,9},{9,10},{10,1... | collective-permute-start | bytes 6291464 | tf_op jit(solution)/shard_map/ppermute | solution.py:20
  22.4 1.6 copy-start.10
  24.0 1.3 copy-start.13
  24.0 1.6 copy-start.9
  36.7 2.0 copy-start.8
  37.9 4.8 copy-start.7
  70.4 0.9 copy-start.3
  71.3 5.0 copy-start
  148.0 0.9 copy-start.3
  148.9 5.1 copy-start
  618.2 2.2 copy-start.12
  618.2 2.9 copy-start.11
  621.2 4.7 copy-start.1
  655.6 4.8 copy-start.2
  655.6 5.0 copy-start.6
  665.2 9.1 %copy-start.14 = (f32[2,512]{1,0:T(2,128)S(1)}, f32[2,512]{1,0:T(2,128)}, u32[]{:S(2)}) copy-start(f32[2,512]{1,0:T(2,128)} %param.18) | copy-start | bytes 12292
  674.3 4.6 copy-start.15
Sparse Core Ops, SparseCore 0:
  36.8 581.3 all-reduce.2
where the time goes:
time: 762 us; the launch traced here: 749 us
  waiting for transfers between devices  409 us (54%)
  local copies, waits for them, and re-layouts  130 us (17%)
  matrix products  92.1 us (12%)
  blocking collectives  52.8 us (7%)
  other arithmetic  36.8 us (5%)
  between operations  13.8 us (2%)
    psum x1, waiting for transfers between devices, shards(): lax.psum((grad_gate, grad_lift, grad_down), 'seq')  409 us
    dynamic_update_slice x4, local copies, waits for them, and re-layouts, window_attention(): return lax.map(one_block, starts).reshape(tokens_here, width_here)  82.9 us
    all_to_all x1, blocking collectives, summed_on_arrival(): lax.all_to_all(tiles, axis, split_axis=0, concat_axis=0, tiled=True)  52.8 us
    dot_general x2, matrix products, orthogonalize(): jnp.einsum('hrc,hcd->hrd', iterate, polynomial, preferred_element_type=jn...  25.2 us
    dynamic_slice x2, local copies, waits for them, and re-layouts, one_block(): lax.dynamic_slice_in_dim(all_keys, start, span_rows, 0)  16 us
  transfers between devices with their start and end apart: 3, of which 1 were waited for; matrix products, arithmetic and copies ran while one was open for 24% of the time, Pallas kernels for 0%

commit v1 on v0

v1 whole, which is shorter than its diff:
```python
import jax
import jax.numpy as jnp
from jax import lax
from jax.experimental import pallas as pl
from jax.experimental.pallas import tpu as pltpu
from jax.sharding import PartitionSpec as P

HEAD = 512
WINDOW = 1024
NS_STEPS = 2
COEF_A = 3.4445
COEF_B = -4.775
COEF_C = 2.0315
EPSILON = 1e-06

CHUNK = 256
BF = jnp.bfloat16
F32 = jnp.float32
MIB = 1 << 20

PLANE = 4
PLANES = 16

ROW_BY_ROW = (((1,), (1,)), ((), ()))
COL_BY_COL = (((0,), (0,)), ((), ()))


def dot(a, b):
    return jnp.dot(a, b, preferred_element_type=F32)


def dot_on(a, b, dims):
    return lax.dot_general(a, b, dims, preferred_element_type=F32)


def any_spec():
    return pl.BlockSpec(memory_space=pl.ANY)


def sigmoid(x):
    return 1.0 / (1.0 + jnp.exp(-x))


def grads_body(where, k_ref, v_ref, rate_ref, gate_ref, lift_ref, down_ref, out_ref, acc, w16):
    step = pl.program_id(0)

    @pl.when(step == 0)
    def _():
        w16[0] = gate_ref[0].astype(BF)
        w16[1] = lift_ref[0].astype(BF)
        w16[2] = down_ref[0].astype(BF)
        acc[...] = jnp.zeros_like(acc)

    keys = k_ref[...]
    rates = jnp.where(where[0] == 0, rate_ref[0:1, :], rate_ref[1:2, :])
    rate_col = jnp.broadcast_to(rates, (128, rates.shape[1])).T[:, :1]
    target = (-rate_col * v_ref[...].astype(F32)).astype(BF)
    gate_pre = dot(keys, w16[0])
    lift_pre = dot(keys, w16[1])
    back_hidden = dot_on(target, w16[2], ROW_BY_ROW)
    sig = sigmoid(gate_pre)
    activated = gate_pre * sig
    hidden = (activated * lift_pre).astype(BF)
    back_gate = (back_hidden * lift_pre * sig * (1.0 + gate_pre * (1.0 - sig))).astype(BF)
    back_lift = (back_hidden * activated).astype(BF)
    acc[0] += dot_on(keys, back_gate, COL_BY_COL)
    acc[1] += dot_on(keys, back_lift, COL_BY_COL)
    acc[2] += dot_on(hidden, target, COL_BY_COL)

    @pl.when(step == pl.num_programs(0) - 1)
    def _():
        for i in range(3):
            out_ref[i * HEAD : (i + 1) * HEAD, :] = acc[i].astype(out_ref.dtype)


def head_grads(which, keys, values, rates, gate, lift, down, dtype):
    tokens = keys.shape[0]
    rows = 256
    weight = pl.BlockSpec((1, HEAD, HEAD), lambda i, w: (w[0], 0, 0))
    token = pl.BlockSpec((rows, HEAD), lambda i, w: (i, w[0]))
    return pl.pallas_call(
        grads_body,
        out_shape=jax.ShapeDtypeStruct((3 * HEAD, HEAD), dtype),
        grid_spec=pltpu.PrefetchScalarGridSpec(
            num_scalar_prefetch=1,
            grid=(tokens // rows,),
            in_specs=[
                token,
                token,
                pl.BlockSpec((2, rows), lambda i, w: (0, i)),
                weight,
                weight,
                weight,
            ],
            out_specs=pl.BlockSpec((3 * HEAD, HEAD), lambda i, w: (0, 0)),
            scratch_shapes=[pltpu.VMEM((3, HEAD, HEAD), F32), pltpu.VMEM((3, HEAD, HEAD), BF)],
        ),
        compiler_params=pltpu.CompilerParams(
            dimension_semantics=("arbitrary",), vmem_limit_bytes=32 * MIB
        ),
        name="head_grads",
    )(which, keys, values, rates, gate, lift, down)


def renew_body(where, g_ref, gate_ref, lift_ref, down_ref, out_ref):
    eye = (
        lax.broadcasted_iota(jnp.int32, (HEAD, HEAD), 0)
        == lax.broadcasted_iota(jnp.int32, (HEAD, HEAD), 1)
    ).astype(F32)
    olds = (gate_ref, lift_ref, down_ref)
    iterates, grams = [], []
    for i in range(3):
        g = g_ref[i * HEAD : (i + 1) * HEAD, :]
        wide = g.astype(F32)
        gram = dot_on(g, g, COL_BY_COL)
        squares = jnp.sum(wide * wide, axis=0, keepdims=True)
        inverse = lax.rsqrt(jnp.sum(squares, axis=1, keepdims=True) + EPSILON)
        iterates.append((wide * inverse).astype(BF))
        grams.append(gram * (inverse * inverse))
    for sweep in range(NS_STEPS):
        polys = []
        for i in range(3):
            half = grams[i].astype(BF)
            square = dot(half, half)
            polys.append((COEF_A * eye + COEF_B * grams[i] + COEF_C * square).astype(BF))
        for i in range(3):
            iterates[i] = dot(iterates[i], polys[i]).astype(BF)
        if sweep + 1 < NS_STEPS:
            for i in range(3):
                grams[i] = dot_on(iterates[i], iterates[i], COL_BY_COL)
    for i in range(3):
        old = olds[i][0]
        change = old - iterates[i].astype(F32)
        old_square = jnp.sum(old * old, axis=0, keepdims=True)
        new_square = jnp.sum(change * change, axis=0, keepdims=True)
        out_ref[i * HEAD : (i + 1) * HEAD, :] = (
            change * jnp.sqrt(old_square / (new_square + EPSILON))
        ).astype(BF)


def renewed_weights(which, grads, gate, lift, down):
    weight = pl.BlockSpec((1, HEAD, HEAD), lambda i, w: (w[0], 0, 0))
    whole = pl.BlockSpec((3 * HEAD, HEAD), lambda i, w: (0, 0))
    return pl.pallas_call(
        renew_body,
        out_shape=jax.ShapeDtypeStruct((3 * HEAD, HEAD), BF),
        grid_spec=pltpu.PrefetchScalarGridSpec(
            num_scalar_prefetch=1,
            grid=(1,),
            in_specs=[whole, weight, weight, weight],
            out_specs=whole,
        ),
        compiler_params=pltpu.CompilerParams(vmem_limit_bytes=48 * MIB),
        name="renewed_weights",
    )(which, grads, gate, lift, down)


def attention_chunk(at, has_edge, queries, keys, values, edge_keys, edge_values, after):
    blocks = WINDOW // CHUNK
    total = blocks + 1
    from_edge = blocks - at
    scale = HEAD ** (-0.5)

    def body(flag, q_ref, *refs):
        k_refs, v_refs, out_ref = refs[:total], refs[total : 2 * total], refs[-1]
        q = q_ref[...]
        row = lax.broadcasted_iota(jnp.int32, (CHUNK, CHUNK), 0)
        col = lax.broadcasted_iota(jnp.int32, (CHUNK, CHUNK), 1)
        scores = [dot_on(q, k_refs[j][...], ROW_BY_ROW) for j in range(total)]
        scores[0] = jnp.where(col > row, scores[0], -jnp.inf)
        scores[-1] = jnp.where(col <= row, scores[-1], -jnp.inf)
        edge_on = flag[0] > 0

        def rowmax(parts):
            best = parts[0]
            for part in parts[1:]:
                best = jnp.maximum(best, part)
            return jnp.max(best, axis=1, keepdims=True)

        own_max = rowmax(scores[from_edge:])
        both_max = jnp.maximum(own_max, rowmax(scores[:from_edge]))
        largest = jnp.where(edge_on, both_max, own_max)
        edge_largest = jnp.where(edge_on, both_max, jnp.inf)
        weights = [
            jnp.exp((scores[j] - (edge_largest if j < from_edge else largest)) * scale)
            for j in range(total)
        ]
        together = weights[0]
        for part in weights[1:]:
            together = together + part
        summed = jnp.sum(together, axis=1, keepdims=True)
        mixed = dot(weights[0].astype(BF), v_refs[0][...])
        for j in range(1, total):
            mixed = mixed + dot(weights[j].astype(BF), v_refs[j][...])
        out_ref[...] = mixed / summed

    def spec(row):
        return pl.BlockSpec((CHUNK, HEAD), lambda h, flag: (row, h))

    rows = [spec(at + j) for j in range(from_edge)] + [spec(j) for j in range(at + 1)]
    key_args = [edge_keys] * from_edge + [keys] * (at + 1)
    value_args = [edge_values] * from_edge + [values] * (at + 1)
    width = queries.shape[1]
    return pl.pallas_call(
        body,
        out_shape=jax.ShapeDtypeStruct((CHUNK, width), F32),
        grid_spec=pltpu.PrefetchScalarGridSpec(
            num_scalar_prefetch=1,
            grid=(width // HEAD,),
            in_specs=[spec(at)] + rows + rows + [any_spec()] * len(after),
            out_specs=pl.BlockSpec((CHUNK, HEAD), lambda h, flag: (0, h)),
        ),
        compiler_params=pltpu.CompilerParams(vmem_limit_bytes=32 * MIB),
        name=f"attention_{at}",
    )(has_edge, queries, *key_args, *value_args, *after)


def tail_body(where, q0, q1, a0, a1, w0, w1, gain, s0, s1, o0, o1, send_ref, own_ref):
    combined = []
    for q_ref, a_ref, w_ref, head in ((q0, a0, w0, where[0]), (q1, a1, w1, 1 - where[0])):
        q = q_ref[...]
        gate = dot(q, w_ref[0:HEAD, :])
        lift = dot(q, w_ref[HEAD : 2 * HEAD, :])
        hidden = (gate * sigmoid(gate) * lift).astype(BF)
        out = dot(hidden, w_ref[2 * HEAD :, :])
        mean_square = jnp.mean(out * out, axis=1, keepdims=True)
        scale = jnp.where(head == 0, gain[0:1, :], gain[1:2, :])
        combined.append((a_ref[...] + out * lax.rsqrt(mean_square + EPSILON) * scale).astype(BF))
    send_ref[...] = (dot(combined[0], s0[...]) + dot(combined[1], s1[...])).astype(BF)
    own_ref[...] = dot(combined[0], o0[...]) + dot(combined[1], o1[...])


def tail_chunk(at, where, queries, attended, mine, theirs, gain, out_weight):
    width = queries.shape[1]
    columns = out_weight.shape[1] // 2
    whole = pl.BlockSpec((3 * HEAD, HEAD), lambda i, w: (0, 0))

    def token(row, mirror):
        return pl.BlockSpec((CHUNK, HEAD), lambda i, w: (row, 1 - w[0] if mirror else w[0]))

    def out_rows(mirror, send):
        return pl.BlockSpec(
            (HEAD, columns),
            lambda i, w: (1 - w[0] if mirror else w[0], 1 - w[1] if send else w[1]),
        )

    block = pl.BlockSpec((CHUNK, columns), lambda i, w: (0, 0))
    return pl.pallas_call(
        tail_body,
        out_shape=(
            jax.ShapeDtypeStruct((CHUNK, columns), BF),
            jax.ShapeDtypeStruct((CHUNK, columns), F32),
        ),
        grid_spec=pltpu.PrefetchScalarGridSpec(
            num_scalar_prefetch=1,
            grid=(1,),
            in_specs=[
                token(at, False),
                token(at, True),
                token(0, False),
                token(0, True),
                whole,
                whole,
                pl.BlockSpec((2, HEAD), lambda i, w: (0, 0)),
                out_rows(False, True),
                out_rows(True, True),
                out_rows(False, False),
                out_rows(True, False),
            ],
            out_specs=[block, block],
        ),
        compiler_params=pltpu.CompilerParams(vmem_limit_bytes=40 * MIB),
        name=f"tail_{at}",
    )(
        where,
        queries,
        queries,
        attended,
        attended,
        mine,
        theirs,
        gain,
        out_weight,
        out_weight,
        out_weight,
        out_weight,
    )


def finish_chunk(at, chunks, own, arrived, before):
    columns = own.shape[1]

    def body(own_ref, arrived_ref, *refs):
        refs[-1][...] = (own_ref[...] + arrived_ref[...].astype(F32)).astype(BF)

    block = pl.BlockSpec((CHUNK, columns), lambda i: (0, 0))
    held = () if before is None else (before,)
    return pl.pallas_call(
        body,
        out_shape=jax.ShapeDtypeStruct((chunks * CHUNK, columns), BF),
        grid=(1,),
        in_specs=[block, block] + [any_spec()] * len(held),
        out_specs=pl.BlockSpec((CHUNK, columns), lambda i: (at, 0)),
        input_output_aliases={2: 0} if held else {},
        name=f"finish_{at}",
    )(own, arrived, *held)


def partner(value, flip):
    count = lax.axis_size("seq")
    return lax.ppermute(value, "seq", [(i, i ^ flip) for i in range(count)])


def over_planes(value):
    groups = [[p * PLANE + r for p in range(PLANES)] for r in range(PLANE)]
    return lax.all_to_all(value, "seq", 0, 0, tiled=True, axis_index_groups=groups)


def shards(
    queries,
    key_rows,
    value_rows,
    token_rates,
    gate_fast,
    lift_fast,
    down_fast,
    memory_gain,
    out_weight,
):
    tokens_here = queries.shape[0]
    chunks = tokens_here // CHUNK
    seq = lax.axis_index("seq")
    core = (seq % 2).astype(jnp.int32)
    head = lax.axis_index("head").astype(jnp.int32)
    where = jnp.stack([core, head])
    mirrored = jnp.stack([1 - core, head])
    has_edge = jnp.where(seq > 0, 1, 0).astype(jnp.int32).reshape(1)

    fast = (gate_fast, lift_fast, down_fast)
    tokens = (key_rows, value_rows, token_rates)
    grads_send = head_grads(mirrored, *tokens, *fast, BF)
    grads_got = partner(grads_send, 1)
    grads_mine = head_grads(where, *tokens, *fast, F32)

    count = lax.axis_size("seq")
    along = [(i, i + 1) for i in range(count - 1)]
    edge_keys, edge_values = lax.ppermute((key_rows, value_rows), "seq", along)

    chip_sum = (grads_mine + grads_got.astype(F32)).astype(BF)
    slices = over_planes(chip_sum.reshape(PLANES, -1, HEAD))
    part = slices.astype(F32).sum(axis=0).astype(BF)
    other = partner(part, 2)
    part = (part.astype(F32) + other.astype(F32)).astype(BF)
    spread = jnp.broadcast_to(part[None], (PLANES, *part.shape))
    grads = over_planes(spread).reshape(3 * HEAD, HEAD)

    weights_mine = renewed_weights(where, grads, *fast)
    weights_theirs = partner(weights_mine, 1)

    head_pair = [(0, 1), (1, 0)]
    owns, arrivals = [], []
    after = ()
    for at in range(chunks):
        if at == 1:
            after = (weights_mine,)
        attended = attention_chunk(
            at, has_edge, queries, key_rows, value_rows, edge_keys, edge_values, after
        )
        send, own = tail_chunk(
            at, where, queries, attended, weights_mine, weights_theirs, memory_gain, out_weight
        )
        owns.append(own)
        arrivals.append(lax.ppermute(send, "head", head_pair))
        after = (send,)
    out = None
    for at in range(chunks):
        out = finish_chunk(at, chunks, owns[at], arrivals[at], out)
    return out


def solution(mesh):
    return jax.shard_map(
        shards,
        mesh=mesh,
        in_specs=(
            P("seq", "head"),
            P("seq", "head"),
            P("seq", "head"),
            P("head", "seq"),
            P("head", None, None),
            P("head", None, None),
            P("head", None, None),
            P("head", None),
            P("head", None),
        ),
        out_specs=P("seq", "head"),
        check_vma=False,
    )
```

time: 762 us -> 194 us (0.25)
  the two profiles are of different devices: /device:TPU:0 before, /device:TPU:32 now
where the time goes in v1:
time: 194 us; the launch traced here: 193 us
  Pallas kernels  74.9 us (39%)
  waiting for transfers between devices  51.2 us (26%)
  blocking collectives  28.6 us (15%)
  starting transfers between devices  20.5 us (11%)
  local copies, waits for them, and re-layouts  16.5 us (9%)
    ppermute x2, waiting for transfers between devices, shards(): edge_keys, edge_values = lax.ppermute((key_rows, value_rows), 'seq', along)  31.2 us
    all_to_all x1, blocking collectives, over_planes(): lax.all_to_all(value, 'seq', 0, 0, tiled=True, axis_index_groups=groups)  28.6 us
    pallas_call x4, Pallas kernels, attention_chunk(): pl.pallas_call(body, out_shape=jax.ShapeDtypeStruct((CHUNK, width), F32),...  21.9 us
    pallas_call x4, Pallas kernels, tail_chunk(): pl.pallas_call(tail_body, out_shape=(jax.ShapeDtypeStruct((CHUNK, columns...  20.1 us
    unnamed x36, local copies, waits for them, and re-layouts  15.3 us
    pallas_call x2, Pallas kernels, head_grads(): pl.pallas_call(grads_body, out_shape=jax.ShapeDtypeStruct((3 * HEAD, HEAD...  14.7 us
    all_to_all x1, waiting for transfers between devices, over_planes(): lax.all_to_all(value, 'seq', 0, 0, tiled=True, axis_index_groups=groups)  14.2 us
    pallas_call x1, Pallas kernels, renewed_weights(): pl.pallas_call(renew_body, out_shape=jax.ShapeDtypeStruct((3 * HEAD, HEAD...  9.2 us
  transfers between devices with their start and end apart: 10, of which 5 were waited for; matrix products, arithmetic and copies ran while one was open for 0% of the time, Pallas kernels for 31%

profile of v1, /device:TPU:32, one launch (start us, length us, event | category | flops | bytes accessed | tf_op | source)
XLA Modules:
  0.0 193.1 jit_solution(11948592167478808651)
XLA Ops:
  0.0 0.1 pad_add_fusion.1.where
  0.1 1.6 copy-done.2
  1.7 1.6 copy-done.5
  3.3 1.6 copy-done.6
  4.9 0.7 copy-done.14
  5.6 7.4 %head_grads.3 = bf16[1536,512]{1,0:T(8,128)(2,1)S(1)} custom-call(s32[2]{0:T(128)S(1)} %pad_add_fusion.1.where, bf16[1024,1024]{1,0:T(8,128)(2,1)} %refs_4_.7, bf16[1024,1024]{1,0:T(8,128)(2,1)} %refs_9_.7, f32[2,1024]{1,0:T(2,128)S(1)} %copy-done.14, f32[2,512,512]{2,1,0:T(8,128)S(1)} %copy-done.2, f32[2,512,512]{2,1,0:T(8,128)S(1)} %copy-done.5, ...), custom_call_target="tpu_custom_call" | custom-call | tf_op jit(solution)/shard_map/head_grads/pallas_call | solution.py:81
  12.9 0.1 collective-permute-start.2
  13.0 0.1 pad_add_fusion.where
  13.1 0.0 copy-done.3
  13.1 0.0 copy-done.15
  13.1 7.3 %head_grads.2 = f32[1536,512]{1,0:T(8,128)S(1)} custom-call(s32[2]{0:T(128)S(1)} %pad_add_fusion.where, bf16[1024,1024]{1,0:T(8,128)(2,1)} %refs_4_.7, bf16[1024,1024]{1,0:T(8,128)(2,1)} %refs_9_.7, f32[2,1024]{1,0:T(2,128)S(1)} %copy-done.15, f32[2,512,512]{2,1,0:T(8,128)S(1)} %copy-done.3, f32[2,512,512]{2,1,0:T(8,128)S(1)} %copy-done.5, ...), custom_call_target="tpu_custom_call" | custom-call | tf_op jit(solution)/shard_map/head_grads/pallas_call | solution.py:81
  20.5 0.0 collective-permute-done.2
  20.5 0.7 add_convert_fusion
  21.2 28.6 %all_to_all.10 = bf16[16,96,512]{2,1,0:T(8,128)(2,1)S(1)} all-to-all(bf16[16,96,512]{2,1,0:T(8,128)(2,1)S(1)} %bitcast.7), channel_id=1, replica_groups={{0,4,8,12,16,20,24,28,32,36,40,44,48,52,56,60},{1,5,9,13,17,21,25,29,33..., dimensions={0} | all-to-all | bytes 3145728 | tf_op jit(solution)/shard_map/all_to_all | solution.py:316
  49.8 0.2 reduce_sum.12
  50.0 1.7 collective-permute-start.3
  51.7 3.0 %collective-permute-done.3 = bf16[96,512]{1,0:T(8,128)(2,1)S(1)} collective-permute-done((bf16[96,512]{1,0:T(8,128)(2,1)S(1)}, bf16[96,512]{1,0:T(8,128)(2,1)S(1)}, u32[]{:S(2)}, u32[]{:S(2)}) %collective-permute-start.3) | collective-permute-done | bytes 98336 | tf_op jit(solution)/shard_map/ppermute | solution.py:311
  54.7 1.3 broadcast_in_dim.2
  56.0 6.2 %all-to-all-start.1 = ((bf16[16,96,512]{2,1,0:T(8,128)(2,1)}), bf16[16,96,512]{2,1,0:T(8,128)(2,1)S(1)}, u32[]{:S(2)}, u32[]{:S(2)}) async-start(bf16[16,96,512]{2,1,0:T(8,128)(2,1)} %broadcast_in_dim.2), calls=%async_computation.1 | async-start | bytes 3145728 | tf_op jit(solution)/shard_map/all_to_all | solution.py:316
  62.2 1.9 collective-permute-start
  64.1 3.6 %collective-permute-start.1 = (bf16[1024,1024]{1,0:T(8,128)(2,1)}, bf16[1024,1024]{1,0:T(8,128)(2,1)}, u32[]{:S(2)}, u32[]{:S(2)}) collective-permute-start(bf16[1024,1024]{1,0:T(8,128)(2,1)} %refs_9_.7), channel_id=1, source_target_pairs={{0,1},{1,2},{2,3},{3,4},{4,5},{5,6},{6,7},{7,8},{8,9},{9,10},{10,1... | collective-permute-start | bytes 6291464 | tf_op jit(solution)/shard_map/ppermute | solution.py:347
  67.7 14.2 %all-to-all-done.1 = bf16[16,96,512]{2,1,0:T(8,128)(2,1)S(1)} async-done(((bf16[16,96,512]{2,1,0:T(8,128)(2,1)}), bf16[16,96,512]{2,1,0:T(8,128)(2,1)S(1)}, u32[]{:S(2)}, u32[]{:S(2)}) %all-to-all-start.1) | async-done | bytes 1572896 | tf_op jit(solution)/shard_map/all_to_all | solution.py:316
  82.0 1.1 copy-done.7
  83.1 1.6 copy-done.4
  84.7 1.4 copy-done.8
  86.1 9.2 %renewed_weights.1.refs_10_.w0 = bf16[1536,512]{1,0:T(8,128)(2,1)} custom-call(s32[2]{0:T(128)S(1)} %pad_add_fusion.where, bf16[1536,512]{1,0:T(8,128)(2,1)S(1)} %bitcast.6, f32[2,512,512]{2,1,0:T(8,128)S(1)} %copy-done.4, f32[2,512,512]{2,1,0:T(8,128)} %lift_ref.5, f32[2,512,512]{2,1,0:T(8,128)} %down_ref.5), custom_call_target="tpu_custom_call" | custom-call | tf_op jit(solution)/shard_map/renewed_weights/pallas_call | solution.py:144
  95.3 0.0 collective-permute-start.4
  95.3 8.7 %collective-permute-done.refs_0_.refs_1_.refs_2_.refs_3_ = bf16[1024,1024]{1,0:T(8,128)(2,1)} collective-permute-done((bf16[1024,1024]{1,0:T(8,128)(2,1)}, bf16[1024,1024]{1,0:T(8,128)(2,1)}, u32[]{:S(2)}, u32[]{:S(2)}) %collective-permute-start) | collective-permute-done | bytes 2097184 | tf_op jit(solution)/shard_map/ppermute | solution.py:347
  104.0 22.5 %collective-permute-done.1.refs_5_.refs_6_.refs_7_.refs_8_ = bf16[1024,1024]{1,0:T(8,128)(2,1)} collective-permute-done((bf16[1024,1024]{1,0:T(8,128)(2,1)}, bf16[1024,1024]{1,0:T(8,128)(2,1)}, u32[]{:S(2)}, u32[]{:S(2)}) %collective-permute-start.1) | collective-permute-done | bytes 2097184 | tf_op jit(solution)/shard_map/ppermute | solution.py:347
  126.5 0.0 copy-done.1
  126.5 5.4 %attention_0.1.a0.a1 = f32[256,1024]{1,0:T(8,128)S(1)} custom-call(s32[1]{0:T(128)} %bitcast.2.flag, bf16[1024,1024]{1,0:T(8,128)(2,1)S(1)} %copy-done.1, bf16[1024,1024]{1,0:T(8,128)(2,1)} %collective-permute-done.refs_0_.refs_1_.refs_2_.refs_3_, bf16[1024,1024]{1,0:T(8,128)(2,1)} %collective-permute-done.refs_0_.refs_1_.refs_2_.refs_3_, ...), custom_call_target="tpu_custom_call" | custom-call | tf_op jit(solution)/shard_map/attention_0/pallas_call | solution.py:204
  131.9 0.0 copy-start
  131.9 0.0 copy-start.13
  132.0 5.6 %attention_1.1.a0.a1 = f32[256,1024]{1,0:T(8,128)S(1)} custom-call(s32[1]{0:T(128)} %bitcast.2.flag, bf16[1024,1024]{1,0:T(8,128)(2,1)S(1)} %copy-done.1, bf16[1024,1024]{1,0:T(8,128)(2,1)} %collective-permute-done.refs_0_.refs_1_.refs_2_.refs_3_, bf16[1024,1024]{1,0:T(8,128)(2,1)} %collective-permute-done.refs_0_.refs_1_.refs_2_.refs_3_, ...), custom_call_target="tpu_custom_call" | custom-call | tf_op jit(solution)/shard_map/attention_1/pallas_call | solution.py:204
  137.6 0.0 collective-permute-done.4.w1
  137.6 0.0 copy-done
  137.6 0.0 copy-done.13
  137.6 5.0 %tail_0.1 = (bf16[256,1024]{1,0:T(8,128)(2,1)S(1)}, f32[256,1024]{1,0:T(8,128)S(1)}) custom-call(s32[2]{0:T(128)S(1)} %pad_add_fusion.where, bf16[1024,1024]{1,0:T(8,128)(2,1)S(1)} %copy-done.1, bf16[1024,1024]{1,0:T(8,128)(2,1)S(1)} %copy-done.1, f32[256,1024]{1,0:T(8,128)S(1)} %attention_0.1.a0.a1, f32[256,1024]{1,0:T(8,128)S(1)} %attention_0.1.a0.a1, ...), custom_call_target="tpu_custom_call" | custom-call | tf_op jit(solution)/shard_map/tail_0/pallas_call | solution.py:248
  142.6 0.0 copy-start.9
  142.6 1.1 copy-done.9
  143.6 2.9 %collective-permute-start.8 = (bf16[256,1024]{1,0:T(8,128)(2,1)S(1)}, bf16[256,1024]{1,0:T(8,128)(2,1)S(1)}, u32[]{:S(2)}, u32[]{:S(2)}) collective-permute-start(bf16[256,1024]{1,0:T(8,128)(2,1)S(1)} %get-tuple-element.20), channel_id=1, source_target_pairs={{0,64},{64,0},{1,65},{65,1},{2,66},{66,2},{3,67},{67,3},{4,68},{68... | collective-permute-start | bytes 1572872 | tf_op jit(solution)/shard_map/ppermute | solution.py:373
  146.5 4.9 %tail_1.1 = (bf16[256,1024]{1,0:T(8,128)(2,1)S(1)}, f32[256,1024]{1,0:T(8,128)S(1)}) custom-call(s32[2]{0:T(128)S(1)} %pad_add_fusion.where, bf16[1024,1024]{1,0:T(8,128)(2,1)S(1)} %copy-done.1, bf16[1024,1024]{1,0:T(8,128)(2,1)S(1)} %copy-done.1, f32[256,1024]{1,0:T(8,128)S(1)} %attention_1.1.a0.a1, f32[256,1024]{1,0:T(8,128)S(1)} %attention_1.1.a0.a1, ...), custom_call_target="tpu_custom_call" | custom-call | tf_op jit(solution)/shard_map/tail_1/pallas_call | solution.py:248
  151.5 0.0 copy-start.10
  151.5 1.0 copy-done.10
  152.5 0.6 collective-permute-start.7
  153.1 5.5 %attention_2.1.a0.a1 = f32[256,1024]{1,0:T(8,128)S(1)} custom-call(s32[1]{0:T(128)} %bitcast.2.flag, bf16[1024,1024]{1,0:T(8,128)(2,1)S(1)} %copy-done.1, bf16[1024,1024]{1,0:T(8,128)(2,1)} %collective-permute-done.refs_0_.refs_1_.refs_2_.refs_3_, bf16[1024,1024]{1,0:T(8,128)(2,1)} %collective-permute-done.refs_0_.refs_1_.refs_2_.refs_3_, ...), custom_call_target="tpu_custom_call" | custom-call | tf_op jit(solution)/shard_map/attention_2/pallas_call | solution.py:204
  158.6 5.0 %tail_2.1 = (bf16[256,1024]{1,0:T(8,128)(2,1)S(1)}, f32[256,1024]{1,0:T(8,128)S(1)}) custom-call(s32[2]{0:T(128)S(1)} %pad_add_fusion.where, bf16[1024,1024]{1,0:T(8,128)(2,1)S(1)} %copy-done.1, bf16[1024,1024]{1,0:T(8,128)(2,1)S(1)} %copy-done.1, f32[256,1024]{1,0:T(8,128)S(1)} %attention_2.1.a0.a1, f32[256,1024]{1,0:T(8,128)S(1)} %attention_2.1.a0.a1, ...), custom_call_target="tpu_custom_call" | custom-call | tf_op jit(solution)/shard_map/tail_2/pallas_call | solution.py:248
  163.5 0.0 copy-start.11
  163.5 1.0 copy-done.11
  164.5 2.9 %collective-permute-start.6 = (bf16[256,1024]{1,0:T(8,128)(2,1)S(1)}, bf16[256,1024]{1,0:T(8,128)(2,1)}, u32[]{:S(2)}, u32[]{:S(2)}) collective-permute-start(bf16[256,1024]{1,0:T(8,128)(2,1)S(1)} %get-tuple-element.14.refs_10_), channel_id=1, source_target_pairs={{0,64},{64,0},{1,65},{65,1},{2,66},{66,2},{3,67},{67,3},{4,68},{68... | collective-permute-start | bytes 1572872 | tf_op jit(solution)/shard_map/ppermute | solution.py:373
  167.4 5.4 %attention_3.1.a0.a1 = f32[256,1024]{1,0:T(8,128)S(1)} custom-call(s32[1]{0:T(128)} %bitcast.2.flag, bf16[1024,1024]{1,0:T(8,128)(2,1)S(1)} %copy-done.1, bf16[1024,1024]{1,0:T(8,128)(2,1)} %collective-permute-done.refs_0_.refs_1_.refs_2_.refs_3_, bf16[1024,1024]{1,0:T(8,128)(2,1)} %refs_4_.7, bf16[1024,1024]{1,0:T(8,128)(2,1)} %refs_4_.7, ...), custom_call_target="tpu_custom_call" | custom-call | tf_op jit(solution)/shard_map/attention_3/pallas_call | solution.py:204
  172.9 5.2 %tail_3.1 = (bf16[256,1024]{1,0:T(8,128)(2,1)}, f32[256,1024]{1,0:T(8,128)S(1)}) custom-call(s32[2]{0:T(128)S(1)} %pad_add_fusion.where, bf16[1024,1024]{1,0:T(8,128)(2,1)S(1)} %copy-done.1, bf16[1024,1024]{1,0:T(8,128)(2,1)S(1)} %copy-done.1, f32[256,1024]{1,0:T(8,128)S(1)} %attention_3.1.a0.a1, f32[256,1024]{1,0:T(8,128)S(1)} %attention_3.1.a0.a1, ...), custom_call_target="tpu_custom_call" | custom-call | tf_op jit(solution)/shard_map/tail_3/pallas_call | solution.py:248
  178.1 1.0 copy-done.12
  179.1 0.6 collective-permute-start.5
  179.7 0.0 collective-permute-done.8.arrived_ref
  179.7 0.8 copy-done.16
  180.5 2.2 %finish_0.1.refs_0_ = bf16[1024,1024]{1,0:T(8,128)(2,1)} custom-call(f32[256,1024]{1,0:T(8,128)} %copy-done.9, bf16[256,1024]{1,0:T(8,128)(2,1)} %copy-done.16), custom_call_target="tpu_custom_call" | custom-call | tf_op jit(solution)/shard_map/finish_0/pallas_call | solution.py:298
  182.8 0.0 collective-permute-done.7.arrived_ref
  182.8 2.2 %finish_1.1.refs_0_ = bf16[1024,1024]{1,0:T(8,128)(2,1)} custom-call(f32[256,1024]{1,0:T(8,128)} %copy-done.10, bf16[256,1024]{1,0:T(8,128)(2,1)} %collective-permute-done.7.arrived_ref, bf16[1024,1024]{1,0:T(8,128)(2,1)} %finish_0.1.refs_0_), custom_call_target="tpu_custom_call", output_to_operand_aliasing={{}: (2, {})} | custom-call | tf_op jit(solution)/shard_map/finish_1/pallas_call | solution.py:298
  185.0 0.0 collective-permute-done.6.arrived_ref
  185.0 2.2 %finish_2.1.refs_0_ = bf16[1024,1024]{1,0:T(8,128)(2,1)} custom-call(f32[256,1024]{1,0:T(8,128)} %copy-done.11, bf16[256,1024]{1,0:T(8,128)(2,1)} %collective-permute-done.6.arrived_ref, bf16[1024,1024]{1,0:T(8,128)(2,1)} %finish_1.1.refs_0_), custom_call_target="tpu_custom_call", output_to_operand_aliasing={{}: (2, {})} | custom-call | tf_op jit(solution)/shard_map/finish_2/pallas_call | solution.py:298
  187.2 2.8 %collective-permute-done.5.arrived_ref = bf16[256,1024]{1,0:T(8,128)(2,1)S(1)} collective-permute-done((bf16[256,1024]{1,0:T(8,128)(2,1)}, bf16[256,1024]{1,0:T(8,128)(2,1)S(1)}, u32[]{:S(2)}, u32[]{:S(2)}) %collective-permute-start.5) | collective-permute-done | bytes 524320 | tf_op jit(solution)/shard_map/ppermute | solution.py:373
  190.0 0.8 copy-done.17
  190.8 2.2 %finish_3.1 = bf16[1024,1024]{1,0:T(8,128)(2,1)} custom-call(f32[256,1024]{1,0:T(8,128)} %copy-done.12, bf16[256,1024]{1,0:T(8,128)(2,1)} %copy-done.17, bf16[1024,1024]{1,0:T(8,128)(2,1)} %finish_2.1.refs_0_), custom_call_target="tpu_custom_call", output_to_operand_aliasing={{}: (2, {})} | custom-call | tf_op jit(solution)/shard_map/finish_3/pallas_call | solution.py:298
  (14 shorter events, 0.0 us)
Async XLA Ops:
  0.1 1.6 copy-start.2
  1.7 1.6 copy-start.5
  3.3 1.6 copy-start.6
  4.9 0.7 copy-start.14
  5.5 7.6 %copy-start.3 = (f32[2,512,512]{2,1,0:T(8,128)S(1)}, f32[2,512,512]{2,1,0:T(8,128)}, u32[]{:S(2)}) copy-start(f32[2,512,512]{2,1,0:T(8,128)} %gate_ref.5) | copy-start | bytes 6291460
  5.5 7.6 %copy-start.15 = (f32[2,1024]{1,0:T(2,128)S(1)}, f32[2,1024]{1,0:T(2,128)}, u32[]{:S(2)}) copy-start(f32[2,1024]{1,0:T(2,128)} %rate_ref.3) | copy-start | bytes 24580
  12.9 7.5 %collective-permute-start.2 = (bf16[1536,512]{1,0:T(8,128)(2,1)S(1)}, bf16[1536,512]{1,0:T(8,128)(2,1)S(1)}, u32[]{:S(2)}, u32[]{:S(2)}) collective-permute-start(bf16[1536,512]{1,0:T(8,128)(2,1)S(1)} %head_grads.3), channel_id=1, source_target_pairs={{0,1},{1,0},{2,3},{3,2},{4,5},{5,4},{6,7},{7,6},{8,9},{9,8},{10,11... | collective-permute-start | bytes 4718600 | tf_op jit(solution)/shard_map/ppermute | solution.py:311
  50.0 4.7 %collective-permute-start.3 = (bf16[96,512]{1,0:T(8,128)(2,1)S(1)}, bf16[96,512]{1,0:T(8,128)(2,1)S(1)}, u32[]{:S(2)}, u32[]{:S(2)}) collective-permute-start(bf16[96,512]{1,0:T(8,128)(2,1)S(1)} %reduce_sum.12), channel_id=1, source_target_pairs={{0,2},{1,3},{2,0},{3,1},{4,6},{5,7},{6,4},{7,5},{8,10},{9,11},{10,... | collective-permute-start | bytes 294920 | tf_op jit(solution)/shard_map/ppermute | solution.py:311
  56.0 25.9 %all-to-all-start.1 = ((bf16[16,96,512]{2,1,0:T(8,128)(2,1)}), bf16[16,96,512]{2,1,0:T(8,128)(2,1)S(1)}, u32[]{:S(2)}, u32[]{:S(2)}) async-start(bf16[16,96,512]{2,1,0:T(8,128)(2,1)} %broadcast_in_dim.2), calls=%async_computation.1 | async-start | bytes 3145728 | tf_op jit(solution)/shard_map/all_to_all | solution.py:316
  62.2 41.8 %collective-permute-start = (bf16[1024,1024]{1,0:T(8,128)(2,1)}, bf16[1024,1024]{1,0:T(8,128)(2,1)}, u32[]{:S(2)}, u32[]{:S(2)}) collective-permute-start(bf16[1024,1024]{1,0:T(8,128)(2,1)} %refs_4_.7), channel_id=1, source_target_pairs={{0,1},{1,2},{2,3},{3,4},{4,5},{5,6},{6,7},{7,8},{8,9},{9,10},{10,1... | collective-permute-start | bytes 6291464 | tf_op jit(solution)/shard_map/ppermute | solution.py:347
  64.1 62.3 %collective-permute-start.1 = (bf16[1024,1024]{1,0:T(8,128)(2,1)}, bf16[1024,1024]{1,0:T(8,128)(2,1)}, u32[]{:S(2)}, u32[]{:S(2)}) collective-permute-start(bf16[1024,1024]{1,0:T(8,128)(2,1)} %refs_9_.7), channel_id=1, source_target_pairs={{0,1},{1,2},{2,3},{3,4},{4,5},{5,6},{6,7},{7,8},{8,9},{9,10},{10,1... | collective-permute-start | bytes 6291464 | tf_op jit(solution)/shard_map/ppermute | solution.py:347
  82.0 1.1 copy-start.7
  83.1 1.6 copy-start.4
  84.7 1.4 copy-start.8
  86.1 40.4 %copy-start.1 = (bf16[1024,1024]{1,0:T(8,128)(2,1)S(1)}, bf16[1024,1024]{1,0:T(8,128)(2,1)}, u32[]{:S(2)}) copy-start(bf16[1024,1024]{1,0:T(8,128)(2,1)} %q1.7) | copy-start | bytes 6291460
  95.3 42.3 %collective-permute-start.4 = (bf16[1536,512]{1,0:T(8,128)(2,1)}, bf16[1536,512]{1,0:T(8,128)(2,1)}, u32[]{:S(2)}, u32[]{:S(2)}) collective-permute-start(bf16[1536,512]{1,0:T(8,128)(2,1)} %renewed_weights.1.refs_10_.w0), channel_id=1, source_target_pairs={{0,1},{1,0},{2,3},{3,2},{4,5},{5,4},{6,7},{7,6},{8,9},{9,8},{10,11... | collective-permute-start | bytes 4718600 | tf_op jit(solution)/shard_map/ppermute | solution.py:311
  131.9 5.6 %copy-start = (bf16[1024,2048]{1,0:T(8,128)(2,1)S(1)}, bf16[1024,2048]{1,0:T(8,128)(2,1)}, u32[]{:S(2)}) copy-start(bf16[1024,2048]{1,0:T(8,128)(2,1)} %o1.7) | copy-start | bytes 12582916
  131.9 5.6 %copy-start.13 = (f32[2,512]{1,0:T(2,128)S(1)}, f32[2,512]{1,0:T(2,128)}, u32[]{:S(2)}) copy-start(f32[2,512]{1,0:T(2,128)} %gain.7) | copy-start | bytes 12292
  142.6 1.1 copy-start.9
  143.6 36.1 %collective-permute-start.8 = (bf16[256,1024]{1,0:T(8,128)(2,1)S(1)}, bf16[256,1024]{1,0:T(8,128)(2,1)S(1)}, u32[]{:S(2)}, u32[]{:S(2)}) collective-permute-start(bf16[256,1024]{1,0:T(8,128)(2,1)S(1)} %get-tuple-element.20), channel_id=1, source_target_pairs={{0,64},{64,0},{1,65},{65,1},{2,66},{66,2},{3,67},{67,3},{4,68},{68... | collective-permute-start | bytes 1572872 | tf_op jit(solution)/shard_map/ppermute | solution.py:373
  151.5 1.0 copy-start.10
  152.5 30.3 %collective-permute-start.7 = (bf16[256,1024]{1,0:T(8,128)(2,1)S(1)}, bf16[256,1024]{1,0:T(8,128)(2,1)}, u32[]{:S(2)}, u32[]{:S(2)}) collective-permute-start(bf16[256,1024]{1,0:T(8,128)(2,1)S(1)} %get-tuple-element.13.refs_10_), channel_id=1, source_target_pairs={{0,64},{64,0},{1,65},{65,1},{2,66},{66,2},{3,67},{67,3},{4,68},{68... | collective-permute-start | bytes 1572872 | tf_op jit(solution)/shard_map/ppermute | solution.py:373
  163.5 1.0 copy-start.11
  164.5 20.5 %collective-permute-start.6 = (bf16[256,1024]{1,0:T(8,128)(2,1)S(1)}, bf16[256,1024]{1,0:T(8,128)(2,1)}, u32[]{:S(2)}, u32[]{:S(2)}) collective-permute-start(bf16[256,1024]{1,0:T(8,128)(2,1)S(1)} %get-tuple-element.14.refs_10_), channel_id=1, source_target_pairs={{0,64},{64,0},{1,65},{65,1},{2,66},{66,2},{3,67},{67,3},{4,68},{68... | collective-permute-start | bytes 1572872 | tf_op jit(solution)/shard_map/ppermute | solution.py:373
  178.1 1.0 copy-start.12
  179.1 10.9 %collective-permute-start.5 = (bf16[256,1024]{1,0:T(8,128)(2,1)}, bf16[256,1024]{1,0:T(8,128)(2,1)S(1)}, u32[]{:S(2)}, u32[]{:S(2)}) collective-permute-start(bf16[256,1024]{1,0:T(8,128)(2,1)} %get-tuple-element.16), channel_id=1, source_target_pairs={{0,64},{64,0},{1,65},{65,1},{2,66},{66,2},{3,67},{67,3},{4,68},{68... | collective-permute-start | bytes 1572872 | tf_op jit(solution)/shard_map/ppermute | solution.py:373
  179.7 0.8 copy-start.16
  190.0 0.8 copy-start.17
